TPU v7x, 256 devices: a whole 4x4x8 slice. The times are simulated.
256 devices in a mesh: layer: 16 (over z, core), dp: 16 (over x, y).
Axes of the slice: x: 4, y: 4, z: 8, core: 2. Of those that a mesh axis runs over, the one named last changes fastest.
Arguments:
- starts: float32 [16, 16, 32, 32, 128], P('layer', 'dp'), may hold values from -6 to 6
- weights: bfloat16 [64, 9, 128, 128], P('layer'), may hold values from -0.1875 to 0.1875
- biases: bfloat16 [64, 128], P('layer'), may hold values from -3 to 3
- adj_ends: float32 [16, 16, 32, 32, 128], P('layer', 'dp'), may hold values from -6 to 6
Outputs:
- block_ends: float32 [16, 16, 32, 32, 128], P('layer', 'dp')
- adjoint_starts: float32 [16, 16, 32, 32, 128], P('layer', 'dp')
- weight_grad: float32 [64, 9, 128, 128], P('layer')
- bias_grad: float32 [64, 128], P('layer')
All inputs are finite; a program needn't handle non-finite values.
Results may differ from a plain program's by a relative error of at most 0.039.
Values may be sent and summed in bfloat16 or wider, within the bound.
No kernel may reach another device: no remote copies, remote signals or barrier semaphores. Data moves between devices by JAX's collectives and lax.ppermute only.
A program may use at most 64 MiB of HBM per device.

v0:
```python
import math
import jax
import jax.numpy as jnp
from jax import lax
from jax.sharding import PartitionSpec as P

step_size = 0.25


def passed_along(x, axis, by):
    peers = lax.axis_size(axis)
    pairs = [(i, i + by) for i in range(peers) if 0 <= i + by < peers]
    return lax.ppermute(x, axis, pairs)


def convolve(rounded, kernel):
    count, map_side, _, channels = rounded.shape
    padded = jnp.pad(rounded, ((0, 0), (1, 1), (1, 1), (0, 0)))
    running = jnp.zeros((count * map_side * map_side, kernel.shape[2]), jnp.float32)
    for tap_index in range(9):
        row_off = tap_index // 3
        col_off = tap_index % 3
        view = padded[:, row_off : row_off + map_side, col_off : col_off + map_side, :].reshape(
            count * map_side * map_side, channels
        )
        running = running + jnp.dot(view, kernel[tap_index], preferred_element_type=jnp.float32)
    return running.reshape(count, map_side, map_side, kernel.shape[2])


def transposed(signal, kernel):
    count, map_side, _, channels = signal.shape
    padded = jnp.pad(signal, ((0, 0), (1, 1), (1, 1), (0, 0)))
    running = jnp.zeros((count * map_side * map_side, kernel.shape[1]), jnp.float32)
    for tap_index in range(9):
        row_off = 2 - tap_index // 3
        col_off = 2 - tap_index % 3
        view = padded[:, row_off : row_off + map_side, col_off : col_off + map_side, :].reshape(
            count * map_side * map_side, channels
        )
        running = running + lax.dot_general(
            view, kernel[tap_index], (((1,), (1,)), ((), ())), preferred_element_type=jnp.float32
        )
    return running.reshape(count, map_side, map_side, kernel.shape[1])


def correlate(rounded, signal):
    count, map_side, _, channels = rounded.shape
    padded = jnp.pad(rounded, ((0, 0), (1, 1), (1, 1), (0, 0)))
    flat_signal = signal.reshape(count * map_side * map_side, signal.shape[3])
    pieces = []
    for tap_index in range(9):
        row_off = tap_index // 3
        col_off = tap_index % 3
        view = padded[:, row_off : row_off + map_side, col_off : col_off + map_side, :].reshape(
            count * map_side * map_side, channels
        )
        pieces.append(
            lax.dot_general(
                view, flat_signal, (((0,), (0,)), ((), ())), preferred_element_type=jnp.float32
            )
        )
    return jnp.stack(pieces)


def activation_of(rounded, kernel, bias_row):
    return jnp.tanh(convolve(rounded, kernel) + bias_row.astype(jnp.float32))


def local(starts, weights, biases, adj_ends):
    layer_index = lax.axis_index("layer")
    blocks = lax.axis_size("layer")
    block_depth = weights.shape[0]
    coarse_step = block_depth * step_size
    map_side = starts.shape[2]
    image_total = starts.shape[1] * lax.axis_size("dp")
    grad_scale = 1.0 / (map_side * math.sqrt(image_total))
    first_state = starts[0]
    adjoint_guess = adj_ends[0]
    first_kernel = weights[0]
    first_bias = biases[0]

    def coarse_apply(current_state, kernel, bias_row):
        return current_state + coarse_step * activation_of(
            current_state.astype(jnp.bfloat16), kernel, bias_row
        )

    current_state = first_state
    for inner_pos in range(block_depth):
        current_state = current_state + step_size * activation_of(
            current_state.astype(jnp.bfloat16), weights[inner_pos], biases[inner_pos]
        )
    relaxed = current_state
    offset = relaxed - coarse_apply(first_state, first_kernel, first_bias)

    def advance(step_index, carried):
        produced = lax.cond(
            layer_index == step_index,
            lambda held: offset + coarse_apply(held, first_kernel, first_bias),
            lambda held: jnp.zeros_like(held),
            carried,
        )
        received = passed_along(produced, "layer", 1)
        return jnp.where(layer_index == step_index + 1, received, carried)

    entry = lax.fori_loop(0, blocks - 1, advance, first_state)
    saved_states = []
    saved_slopes = []
    current_state = entry
    for inner_pos in range(block_depth):
        rounded = current_state.astype(jnp.bfloat16)
        saved_states.append(rounded)
        activation = activation_of(rounded, weights[inner_pos], biases[inner_pos])
        saved_slopes.append(1.0 - activation * activation)
        current_state = current_state + step_size * activation
    adjoint = adjoint_guess
    for inner_pos in reversed(range(block_depth)):
        signal = (saved_slopes[inner_pos] * adjoint).astype(jnp.bfloat16)
        adjoint = adjoint + step_size * transposed(signal, weights[inner_pos])
    backed = adjoint

    def coarse_adjoint(difference):
        signal = (saved_slopes[0] * difference).astype(jnp.bfloat16)
        return difference + coarse_step * transposed(signal, first_kernel)

    def retreat(step_index, carried):
        sender = blocks - 1 - step_index
        produced = lax.cond(
            layer_index == sender,
            lambda held: backed + coarse_adjoint(held - adjoint_guess),
            lambda held: jnp.zeros_like(held),
            carried,
        )
        received = passed_along(produced.astype(jnp.bfloat16), "layer", -1).astype(produced.dtype)
        return jnp.where(layer_index == sender - 1, received, carried)

    exit_adjoint = lax.fori_loop(0, blocks - 1, retreat, adjoint_guess)
    kernel_grads = [None] * block_depth
    bias_grads = [None] * block_depth
    adjoint = exit_adjoint
    for inner_pos in reversed(range(block_depth)):
        signal = (saved_slopes[inner_pos] * adjoint).astype(jnp.bfloat16)
        kernel_part = correlate(saved_states[inner_pos], signal) * grad_scale
        bias_part = jnp.sum(signal.astype(jnp.float32), axis=(0, 1, 2)) * grad_scale
        kernel_grads[inner_pos] = kernel_part
        bias_grads[inner_pos] = bias_part
        adjoint = adjoint + step_size * transposed(signal, weights[inner_pos])
    kernel_stack = jnp.stack(kernel_grads)
    bias_stack = jnp.stack(bias_grads)
    kernel_stack, bias_stack = (
        lax.psum(kernel_stack.astype(jnp.bfloat16), "dp").astype(jnp.float32),
        lax.psum(bias_stack.astype(jnp.bfloat16), "dp").astype(jnp.float32),
    )
    return (current_state[None], adjoint[None], kernel_stack, bias_stack)


def solution(mesh):
    in_specs = (
        P("layer", "dp", None, None, None),
        P("layer", None, None, None),
        P("layer", None),
        P("layer", "dp", None, None, None),
    )
    out_specs = (
        P("layer", "dp", None, None, None),
        P("layer", "dp", None, None, None),
        P("layer", None, None, None),
        P("layer", None),
    )
    return jax.shard_map(local, mesh=mesh, in_specs=in_specs, out_specs=out_specs, check_vma=False)
```

profile of v0, /device:TPU:32, one launch (start us, length us, event | category | flops | bytes accessed | tf_op | source)
XLA Modules:
  0.0 527.7 jit_solution(16567710539062359884)
XLA Ops:
  22.3 178.5 %while.30 = (s32[]{:T(128)}, f32[1,32,32,128]{3,2,1,0:T(8,128)S(1)}, s32[]{:T(128)}, bf16[9,128,128]{2,1,0:T(8,128)(2,1)S(1)}, bf16[128]{0:T(256)(128)(2,1)S(1)}, /*index=5*/f32[1,32,32,128]{3,2,1,0:T(8,128)S(1)}, s32[]{:T(128)}) while((s32[]{:T(128)}, f32[1,32,32,128]{3,2,1,0:T(8,128)S(1)}, s32[]{:T(128)}, ...), condition=%wide.region_3.4_spmd, body=%wide.region_0.3_spmd.sunk | while | flops 303693952 | bytes 22578640 | solution.py:105
  25.1 8.8 %collective-permute-done = f32[1,32,32,128]{3,2,1,0:T(8,128)S(1)} collective-permute-done((f32[1,32,32,128]{3,2,1,0:T(8,128)}, f32[1,32,32,128]{3,2,1,0:T(8,128)S(1)}, u32[]{:S(2)}, u32[]{:S(2)}) %collective-permute-start) | collective-permute-done | bytes 524320 | tf_op jit(solution)/shard_map/while/body/eval_jaxpr/ppermute | solution.py:13
  36.9 8.8 %collective-permute-done = f32[1,32,32,128]{3,2,1,0:T(8,128)S(1)} collective-permute-done((f32[1,32,32,128]{3,2,1,0:T(8,128)}, f32[1,32,32,128]{3,2,1,0:T(8,128)S(1)}, u32[]{:S(2)}, u32[]{:S(2)}) %collective-permute-start) | collective-permute-done | bytes 524320 | tf_op jit(solution)/shard_map/while/body/eval_jaxpr/ppermute | solution.py:13
  45.8 2.5 conditional.4
  51.0 8.8 %collective-permute-done = f32[1,32,32,128]{3,2,1,0:T(8,128)S(1)} collective-permute-done((f32[1,32,32,128]{3,2,1,0:T(8,128)}, f32[1,32,32,128]{3,2,1,0:T(8,128)S(1)}, u32[]{:S(2)}, u32[]{:S(2)}) %collective-permute-start) | collective-permute-done | bytes 524320 | tf_op jit(solution)/shard_map/while/body/eval_jaxpr/ppermute | solution.py:13
  62.8 8.8 %collective-permute-done = f32[1,32,32,128]{3,2,1,0:T(8,128)S(1)} collective-permute-done((f32[1,32,32,128]{3,2,1,0:T(8,128)}, f32[1,32,32,128]{3,2,1,0:T(8,128)S(1)}, u32[]{:S(2)}, u32[]{:S(2)}) %collective-permute-start) | collective-permute-done | bytes 524320 | tf_op jit(solution)/shard_map/while/body/eval_jaxpr/ppermute | solution.py:13
  72.6 1.9 collective-permute-start
  74.5 8.8 %collective-permute-done = f32[1,32,32,128]{3,2,1,0:T(8,128)S(1)} collective-permute-done((f32[1,32,32,128]{3,2,1,0:T(8,128)}, f32[1,32,32,128]{3,2,1,0:T(8,128)S(1)}, u32[]{:S(2)}, u32[]{:S(2)}) %collective-permute-start) | collective-permute-done | bytes 524320 | tf_op jit(solution)/shard_map/while/body/eval_jaxpr/ppermute | solution.py:13
  84.3 1.9 collective-permute-start
  86.2 8.8 %collective-permute-done = f32[1,32,32,128]{3,2,1,0:T(8,128)S(1)} collective-permute-done((f32[1,32,32,128]{3,2,1,0:T(8,128)}, f32[1,32,32,128]{3,2,1,0:T(8,128)S(1)}, u32[]{:S(2)}, u32[]{:S(2)}) %collective-permute-start) | collective-permute-done | bytes 524320 | tf_op jit(solution)/shard_map/while/body/eval_jaxpr/ppermute | solution.py:13
  96.0 1.9 collective-permute-start
  98.0 8.8 %collective-permute-done = f32[1,32,32,128]{3,2,1,0:T(8,128)S(1)} collective-permute-done((f32[1,32,32,128]{3,2,1,0:T(8,128)}, f32[1,32,32,128]{3,2,1,0:T(8,128)S(1)}, u32[]{:S(2)}, u32[]{:S(2)}) %collective-permute-start) | collective-permute-done | bytes 524320 | tf_op jit(solution)/shard_map/while/body/eval_jaxpr/ppermute | solution.py:13
  107.8 1.9 collective-permute-start
  109.7 8.8 %collective-permute-done = f32[1,32,32,128]{3,2,1,0:T(8,128)S(1)} collective-permute-done((f32[1,32,32,128]{3,2,1,0:T(8,128)}, f32[1,32,32,128]{3,2,1,0:T(8,128)S(1)}, u32[]{:S(2)}, u32[]{:S(2)}) %collective-permute-start) | collective-permute-done | bytes 524320 | tf_op jit(solution)/shard_map/while/body/eval_jaxpr/ppermute | solution.py:13
  119.5 1.9 collective-permute-start
  121.4 8.8 %collective-permute-done = f32[1,32,32,128]{3,2,1,0:T(8,128)S(1)} collective-permute-done((f32[1,32,32,128]{3,2,1,0:T(8,128)}, f32[1,32,32,128]{3,2,1,0:T(8,128)S(1)}, u32[]{:S(2)}, u32[]{:S(2)}) %collective-permute-start) | collective-permute-done | bytes 524320 | tf_op jit(solution)/shard_map/while/body/eval_jaxpr/ppermute | solution.py:13
  131.2 1.9 collective-permute-start
  133.1 8.8 %collective-permute-done = f32[1,32,32,128]{3,2,1,0:T(8,128)S(1)} collective-permute-done((f32[1,32,32,128]{3,2,1,0:T(8,128)}, f32[1,32,32,128]{3,2,1,0:T(8,128)S(1)}, u32[]{:S(2)}, u32[]{:S(2)}) %collective-permute-start) | collective-permute-done | bytes 524320 | tf_op jit(solution)/shard_map/while/body/eval_jaxpr/ppermute | solution.py:13
  142.9 1.9 collective-permute-start
  144.9 8.8 %collective-permute-done = f32[1,32,32,128]{3,2,1,0:T(8,128)S(1)} collective-permute-done((f32[1,32,32,128]{3,2,1,0:T(8,128)}, f32[1,32,32,128]{3,2,1,0:T(8,128)S(1)}, u32[]{:S(2)}, u32[]{:S(2)}) %collective-permute-start) | collective-permute-done | bytes 524320 | tf_op jit(solution)/shard_map/while/body/eval_jaxpr/ppermute | solution.py:13
  156.6 8.8 %collective-permute-done = f32[1,32,32,128]{3,2,1,0:T(8,128)S(1)} collective-permute-done((f32[1,32,32,128]{3,2,1,0:T(8,128)}, f32[1,32,32,128]{3,2,1,0:T(8,128)S(1)}, u32[]{:S(2)}, u32[]{:S(2)}) %collective-permute-start) | collective-permute-done | bytes 524320 | tf_op jit(solution)/shard_map/while/body/eval_jaxpr/ppermute | solution.py:13
  168.3 8.8 %collective-permute-done = f32[1,32,32,128]{3,2,1,0:T(8,128)S(1)} collective-permute-done((f32[1,32,32,128]{3,2,1,0:T(8,128)}, f32[1,32,32,128]{3,2,1,0:T(8,128)S(1)}, u32[]{:S(2)}, u32[]{:S(2)}) %collective-permute-start) | collective-permute-done | bytes 524320 | tf_op jit(solution)/shard_map/while/body/eval_jaxpr/ppermute | solution.py:13
  180.0 8.8 %collective-permute-done = f32[1,32,32,128]{3,2,1,0:T(8,128)S(1)} collective-permute-done((f32[1,32,32,128]{3,2,1,0:T(8,128)}, f32[1,32,32,128]{3,2,1,0:T(8,128)S(1)}, u32[]{:S(2)}, u32[]{:S(2)}) %collective-permute-start) | collective-permute-done | bytes 524320 | tf_op jit(solution)/shard_map/while/body/eval_jaxpr/ppermute | solution.py:13
  191.8 8.8 %collective-permute-done = f32[1,32,32,128]{3,2,1,0:T(8,128)S(1)} collective-permute-done((f32[1,32,32,128]{3,2,1,0:T(8,128)}, f32[1,32,32,128]{3,2,1,0:T(8,128)S(1)}, u32[]{:S(2)}, u32[]{:S(2)}) %collective-permute-start) | collective-permute-done | bytes 524320 | tf_op jit(solution)/shard_map/while/body/eval_jaxpr/ppermute | solution.py:13
  223.7 168.4 %while.31 = (s32[]{:T(128)}, f32[1,32,32,128]{3,2,1,0:T(8,128)S(1)}, s32[]{:T(128)}, f32[1,32,32,128]{3,2,1,0:T(8,128)S(1)}, f32[1,32,32,128]{3,2,1,0:T(8,128)S(...) while((s32[]{:T(128)}, ...), condition=%wide.region_7.8_spmd, body=%wide.region_4.7_spmd.sunk | while | flops 304087040 | bytes 23626020 | solution.py:136
  226.4 4.2 collective-permute-done.1
  231.5 3.7 collective-permute-start.1
  235.2 4.2 collective-permute-done.1
  240.3 3.7 collective-permute-start.1
  244.0 4.7 collective-permute-done.1
  249.6 3.2 collective-permute-start.1
  252.8 6.6 %collective-permute-done.1 = bf16[1,32,32,128]{3,2,1,0:T(8,128)(2,1)S(1)} collective-permute-done((bf16[1,32,32,128]{3,2,1,0:T(8,128)(2,1)}, bf16[1,32,32,128]{3,2,1,0:T(8,128)(2,1)S(1)}, u32[]{:S(2)}, u32[]{:S(2)}) %collective-permute-start.1) | collective-permute-done | bytes 262176 | tf_op jit(solution)/shard_map/while/body/eval_jaxpr/ppermute | solution.py:13
  262.2 9.5 %collective-permute-done.1 = bf16[1,32,32,128]{3,2,1,0:T(8,128)(2,1)S(1)} collective-permute-done((bf16[1,32,32,128]{3,2,1,0:T(8,128)(2,1)}, bf16[1,32,32,128]{3,2,1,0:T(8,128)(2,1)S(1)}, u32[]{:S(2)}, u32[]{:S(2)}) %collective-permute-start.1) | collective-permute-done | bytes 262176 | tf_op jit(solution)/shard_map/while/body/eval_jaxpr/ppermute | solution.py:13
  274.6 7.8 %collective-permute-done.1 = bf16[1,32,32,128]{3,2,1,0:T(8,128)(2,1)S(1)} collective-permute-done((bf16[1,32,32,128]{3,2,1,0:T(8,128)(2,1)}, bf16[1,32,32,128]{3,2,1,0:T(8,128)(2,1)S(1)}, u32[]{:S(2)}, u32[]{:S(2)}) %collective-permute-start.1) | collective-permute-done | bytes 262176 | tf_op jit(solution)/shard_map/while/body/eval_jaxpr/ppermute | solution.py:13
  285.2 7.2 %collective-permute-done.1 = bf16[1,32,32,128]{3,2,1,0:T(8,128)(2,1)S(1)} collective-permute-done((bf16[1,32,32,128]{3,2,1,0:T(8,128)(2,1)}, bf16[1,32,32,128]{3,2,1,0:T(8,128)(2,1)S(1)}, u32[]{:S(2)}, u32[]{:S(2)}) %collective-permute-start.1) | collective-permute-done | bytes 262176 | tf_op jit(solution)/shard_map/while/body/eval_jaxpr/ppermute | solution.py:13
  295.3 7.2 %collective-permute-done.1 = bf16[1,32,32,128]{3,2,1,0:T(8,128)(2,1)S(1)} collective-permute-done((bf16[1,32,32,128]{3,2,1,0:T(8,128)(2,1)}, bf16[1,32,32,128]{3,2,1,0:T(8,128)(2,1)S(1)}, u32[]{:S(2)}, u32[]{:S(2)}) %collective-permute-start.1) | collective-permute-done | bytes 262176 | tf_op jit(solution)/shard_map/while/body/eval_jaxpr/ppermute | solution.py:13
  305.3 7.2 %collective-permute-done.1 = bf16[1,32,32,128]{3,2,1,0:T(8,128)(2,1)S(1)} collective-permute-done((bf16[1,32,32,128]{3,2,1,0:T(8,128)(2,1)}, bf16[1,32,32,128]{3,2,1,0:T(8,128)(2,1)S(1)}, u32[]{:S(2)}, u32[]{:S(2)}) %collective-permute-start.1) | collective-permute-done | bytes 262176 | tf_op jit(solution)/shard_map/while/body/eval_jaxpr/ppermute | solution.py:13
  315.3 7.2 %collective-permute-done.1 = bf16[1,32,32,128]{3,2,1,0:T(8,128)(2,1)S(1)} collective-permute-done((bf16[1,32,32,128]{3,2,1,0:T(8,128)(2,1)}, bf16[1,32,32,128]{3,2,1,0:T(8,128)(2,1)S(1)}, u32[]{:S(2)}, u32[]{:S(2)}) %collective-permute-start.1) | collective-permute-done | bytes 262176 | tf_op jit(solution)/shard_map/while/body/eval_jaxpr/ppermute | solution.py:13
  325.4 7.2 %collective-permute-done.1 = bf16[1,32,32,128]{3,2,1,0:T(8,128)(2,1)S(1)} collective-permute-done((bf16[1,32,32,128]{3,2,1,0:T(8,128)(2,1)}, bf16[1,32,32,128]{3,2,1,0:T(8,128)(2,1)S(1)}, u32[]{:S(2)}, u32[]{:S(2)}) %collective-permute-start.1) | collective-permute-done | bytes 262176 | tf_op jit(solution)/shard_map/while/body/eval_jaxpr/ppermute | solution.py:13
  335.4 7.2 %collective-permute-done.1 = bf16[1,32,32,128]{3,2,1,0:T(8,128)(2,1)S(1)} collective-permute-done((bf16[1,32,32,128]{3,2,1,0:T(8,128)(2,1)}, bf16[1,32,32,128]{3,2,1,0:T(8,128)(2,1)S(1)}, u32[]{:S(2)}, u32[]{:S(2)}) %collective-permute-start.1) | collective-permute-done | bytes 262176 | tf_op jit(solution)/shard_map/while/body/eval_jaxpr/ppermute | solution.py:13
  345.4 23.9 %collective-permute-done.1 = bf16[1,32,32,128]{3,2,1,0:T(8,128)(2,1)S(1)} collective-permute-done((bf16[1,32,32,128]{3,2,1,0:T(8,128)(2,1)}, bf16[1,32,32,128]{3,2,1,0:T(8,128)(2,1)S(1)}, u32[]{:S(2)}, u32[]{:S(2)}) %collective-permute-start.1) | collective-permute-done | bytes 262176 | tf_op jit(solution)/shard_map/while/body/eval_jaxpr/ppermute | solution.py:13
  369.5 3.3 conditional.5
  375.4 4.2 collective-permute-done.1
  380.6 7.0 %collective-permute-start.1 = (bf16[1,32,32,128]{3,2,1,0:T(8,128)(2,1)}, bf16[1,32,32,128]{3,2,1,0:T(8,128)(2,1)S(1)}, u32[]{:S(2)}, u32[]{:S(2)}) collective-permute-start(bf16[1,32,32,128]{3,2,1,0:T(8,128)(2,1)} %copy-done.12), channel_id=1, source_target_pairs={{16,0},{32,16},{48,32},{64,48},{80,64},{96,80},{112,96},{128,112},... | collective-permute-start | bytes 786440 | tf_op jit(solution)/shard_map/while/body/eval_jaxpr/ppermute | solution.py:13
  387.6 4.2 collective-permute-done.1
  417.9 40.9 %psum.15 = bf16[4,128]{1,0:T(4,128)(2,1)S(1)} all-reduce(bf16[4,128]{1,0:T(4,128)(2,1)S(1)} %pad_maximum_fusion.1), channel_id=1, replica_groups=mesh['layer'=16,'dp'=16] {'dp'}, use_global_device_ids=true, to_apply=%region_13.14 | all-reduce | flops 512 | bytes 2048 | tf_op jit(solution)/shard_map/psum | solution.py:151
  464.4 53.4 %all-reduce.20.cloned.1.call-done = bf16[4,9,128,128]{3,2,1,0:T(8,128)(2,1)} async-done(((bf16[4,9,128,128]{3,2,1,0:T(8,128)(2,1)}), bf16[4,9,128,128]{3,2,1,0:T(8,128)(2,1)}) %all-reduce.20.cloned.1.call-update) | async-done | bytes 1179664 | tf_op jit(solution)/shard_map/psum | solution.py:150
  517.9 3.0 convert_element_type.313
  (479 shorter events, 138.6 us)
Async XLA Ops:
  7.2 510.7 %all-reduce.20.cloned.1.call-start = ((), (), s32[]{:S(2)}) async-start(), calls=%async_computation | async-start | bytes 2359296 | tf_op jit(solution)/shard_map/psum | solution.py:150
  8.3 1.3 copy-start.1
  12.0 2.4 copy-start.10
  14.7 2.3 copy-start.15
  19.3 1.2 copy-start.31
  19.3 1.5 copy-start.29
  20.8 1.2 copy-start.16
  23.2 10.7 %collective-permute-start = (f32[1,32,32,128]{3,2,1,0:T(8,128)}, f32[1,32,32,128]{3,2,1,0:T(8,128)S(1)}, u32[]{:S(2)}, u32[]{:S(2)}) collective-permute-start(f32[1,32,32,128]{3,2,1,0:T(8,128)} %copy-done.5), channel_id=1, source_target_pairs={{0,16},{16,32},{32,48},{48,64},{64,80},{80,96},{96,112},{112,128},... | collective-permute-start | bytes 1572872 | tf_op jit(solution)/shard_map/while/body/eval_jaxpr/ppermute | solution.py:13
  34.9 10.8 %collective-permute-start = (f32[1,32,32,128]{3,2,1,0:T(8,128)}, f32[1,32,32,128]{3,2,1,0:T(8,128)S(1)}, u32[]{:S(2)}, u32[]{:S(2)}) collective-permute-start(f32[1,32,32,128]{3,2,1,0:T(8,128)} %copy-done.5), channel_id=1, source_target_pairs={{0,16},{16,32},{32,48},{48,64},{64,80},{80,96},{96,112},{112,128},... | collective-permute-start | bytes 1572872 | tf_op jit(solution)/shard_map/while/body/eval_jaxpr/ppermute | solution.py:13
  49.1 10.7 %collective-permute-start = (f32[1,32,32,128]{3,2,1,0:T(8,128)}, f32[1,32,32,128]{3,2,1,0:T(8,128)S(1)}, u32[]{:S(2)}, u32[]{:S(2)}) collective-permute-start(f32[1,32,32,128]{3,2,1,0:T(8,128)} %copy-done.5), channel_id=1, source_target_pairs={{0,16},{16,32},{32,48},{48,64},{64,80},{80,96},{96,112},{112,128},... | collective-permute-start | bytes 1572872 | tf_op jit(solution)/shard_map/while/body/eval_jaxpr/ppermute | solution.py:13
  60.8 10.7 %collective-permute-start = (f32[1,32,32,128]{3,2,1,0:T(8,128)}, f32[1,32,32,128]{3,2,1,0:T(8,128)S(1)}, u32[]{:S(2)}, u32[]{:S(2)}) collective-permute-start(f32[1,32,32,128]{3,2,1,0:T(8,128)} %copy-done.5), channel_id=1, source_target_pairs={{0,16},{16,32},{32,48},{48,64},{64,80},{80,96},{96,112},{112,128},... | collective-permute-start | bytes 1572872 | tf_op jit(solution)/shard_map/while/body/eval_jaxpr/ppermute | solution.py:13
  72.6 10.7 %collective-permute-start = (f32[1,32,32,128]{3,2,1,0:T(8,128)}, f32[1,32,32,128]{3,2,1,0:T(8,128)S(1)}, u32[]{:S(2)}, u32[]{:S(2)}) collective-permute-start(f32[1,32,32,128]{3,2,1,0:T(8,128)} %copy-done.5), channel_id=1, source_target_pairs={{0,16},{16,32},{32,48},{48,64},{64,80},{80,96},{96,112},{112,128},... | collective-permute-start | bytes 1572872 | tf_op jit(solution)/shard_map/while/body/eval_jaxpr/ppermute | solution.py:13
  84.3 10.7 %collective-permute-start = (f32[1,32,32,128]{3,2,1,0:T(8,128)}, f32[1,32,32,128]{3,2,1,0:T(8,128)S(1)}, u32[]{:S(2)}, u32[]{:S(2)}) collective-permute-start(f32[1,32,32,128]{3,2,1,0:T(8,128)} %copy-done.5), channel_id=1, source_target_pairs={{0,16},{16,32},{32,48},{48,64},{64,80},{80,96},{96,112},{112,128},... | collective-permute-start | bytes 1572872 | tf_op jit(solution)/shard_map/while/body/eval_jaxpr/ppermute | solution.py:13
  96.0 10.7 %collective-permute-start = (f32[1,32,32,128]{3,2,1,0:T(8,128)}, f32[1,32,32,128]{3,2,1,0:T(8,128)S(1)}, u32[]{:S(2)}, u32[]{:S(2)}) collective-permute-start(f32[1,32,32,128]{3,2,1,0:T(8,128)} %copy-done.5), channel_id=1, source_target_pairs={{0,16},{16,32},{32,48},{48,64},{64,80},{80,96},{96,112},{112,128},... | collective-permute-start | bytes 1572872 | tf_op jit(solution)/shard_map/while/body/eval_jaxpr/ppermute | solution.py:13
  107.8 10.7 %collective-permute-start = (f32[1,32,32,128]{3,2,1,0:T(8,128)}, f32[1,32,32,128]{3,2,1,0:T(8,128)S(1)}, u32[]{:S(2)}, u32[]{:S(2)}) collective-permute-start(f32[1,32,32,128]{3,2,1,0:T(8,128)} %copy-done.5), channel_id=1, source_target_pairs={{0,16},{16,32},{32,48},{48,64},{64,80},{80,96},{96,112},{112,128},... | collective-permute-start | bytes 1572872 | tf_op jit(solution)/shard_map/while/body/eval_jaxpr/ppermute | solution.py:13
  119.5 10.7 %collective-permute-start = (f32[1,32,32,128]{3,2,1,0:T(8,128)}, f32[1,32,32,128]{3,2,1,0:T(8,128)S(1)}, u32[]{:S(2)}, u32[]{:S(2)}) collective-permute-start(f32[1,32,32,128]{3,2,1,0:T(8,128)} %copy-done.5), channel_id=1, source_target_pairs={{0,16},{16,32},{32,48},{48,64},{64,80},{80,96},{96,112},{112,128},... | collective-permute-start | bytes 1572872 | tf_op jit(solution)/shard_map/while/body/eval_jaxpr/ppermute | solution.py:13
  131.2 10.7 %collective-permute-start = (f32[1,32,32,128]{3,2,1,0:T(8,128)}, f32[1,32,32,128]{3,2,1,0:T(8,128)S(1)}, u32[]{:S(2)}, u32[]{:S(2)}) collective-permute-start(f32[1,32,32,128]{3,2,1,0:T(8,128)} %copy-done.5), channel_id=1, source_target_pairs={{0,16},{16,32},{32,48},{48,64},{64,80},{80,96},{96,112},{112,128},... | collective-permute-start | bytes 1572872 | tf_op jit(solution)/shard_map/while/body/eval_jaxpr/ppermute | solution.py:13
  142.9 10.7 %collective-permute-start = (f32[1,32,32,128]{3,2,1,0:T(8,128)}, f32[1,32,32,128]{3,2,1,0:T(8,128)S(1)}, u32[]{:S(2)}, u32[]{:S(2)}) collective-permute-start(f32[1,32,32,128]{3,2,1,0:T(8,128)} %copy-done.5), channel_id=1, source_target_pairs={{0,16},{16,32},{32,48},{48,64},{64,80},{80,96},{96,112},{112,128},... | collective-permute-start | bytes 1572872 | tf_op jit(solution)/shard_map/while/body/eval_jaxpr/ppermute | solution.py:13
  154.7 10.7 %collective-permute-start = (f32[1,32,32,128]{3,2,1,0:T(8,128)}, f32[1,32,32,128]{3,2,1,0:T(8,128)S(1)}, u32[]{:S(2)}, u32[]{:S(2)}) collective-permute-start(f32[1,32,32,128]{3,2,1,0:T(8,128)} %copy-done.5), channel_id=1, source_target_pairs={{0,16},{16,32},{32,48},{48,64},{64,80},{80,96},{96,112},{112,128},... | collective-permute-start | bytes 1572872 | tf_op jit(solution)/shard_map/while/body/eval_jaxpr/ppermute | solution.py:13
  166.4 10.7 %collective-permute-start = (f32[1,32,32,128]{3,2,1,0:T(8,128)}, f32[1,32,32,128]{3,2,1,0:T(8,128)S(1)}, u32[]{:S(2)}, u32[]{:S(2)}) collective-permute-start(f32[1,32,32,128]{3,2,1,0:T(8,128)} %copy-done.5), channel_id=1, source_target_pairs={{0,16},{16,32},{32,48},{48,64},{64,80},{80,96},{96,112},{112,128},... | collective-permute-start | bytes 1572872 | tf_op jit(solution)/shard_map/while/body/eval_jaxpr/ppermute | solution.py:13
  178.1 10.7 %collective-permute-start = (f32[1,32,32,128]{3,2,1,0:T(8,128)}, f32[1,32,32,128]{3,2,1,0:T(8,128)S(1)}, u32[]{:S(2)}, u32[]{:S(2)}) collective-permute-start(f32[1,32,32,128]{3,2,1,0:T(8,128)} %copy-done.5), channel_id=1, source_target_pairs={{0,16},{16,32},{32,48},{48,64},{64,80},{80,96},{96,112},{112,128},... | collective-permute-start | bytes 1572872 | tf_op jit(solution)/shard_map/while/body/eval_jaxpr/ppermute | solution.py:13
  189.8 10.7 %collective-permute-start = (f32[1,32,32,128]{3,2,1,0:T(8,128)}, f32[1,32,32,128]{3,2,1,0:T(8,128)S(1)}, u32[]{:S(2)}, u32[]{:S(2)}) collective-permute-start(f32[1,32,32,128]{3,2,1,0:T(8,128)} %copy-done.5), channel_id=1, source_target_pairs={{0,16},{16,32},{32,48},{48,64},{64,80},{80,96},{96,112},{112,128},... | collective-permute-start | bytes 1572872 | tf_op jit(solution)/shard_map/while/body/eval_jaxpr/ppermute | solution.py:13
  200.9 1.2 copy-start.17
  203.3 1.2 copy-start.19
  205.6 13.2 %copy-start.6 = (f32[1024,128]{1,0:T(8,128)}, f32[1024,128]{1,0:T(8,128)S(1)}, u32[]{:S(2)}) copy-start(f32[1024,128]{1,0:T(8,128)S(1)} %convolution_add_fusion.96) | copy-start | bytes 1572868
  205.8 1.2 copy-start.21
  205.8 2.3 copy-start.13
  208.1 7.9 %copy-start.3 = (f32[1024,128]{1,0:T(8,128)}, f32[1024,128]{1,0:T(8,128)S(1)}, u32[]{:S(2)}) copy-start(f32[1024,128]{1,0:T(8,128)S(1)} %convolution_add_fusion.88) | copy-start | bytes 1572868
  208.2 1.2 copy-start.23
  224.4 6.1 %collective-permute-start.1 = (bf16[1,32,32,128]{3,2,1,0:T(8,128)(2,1)}, bf16[1,32,32,128]{3,2,1,0:T(8,128)(2,1)S(1)}, u32[]{:S(2)}, u32[]{:S(2)}) collective-permute-start(bf16[1,32,32,128]{3,2,1,0:T(8,128)(2,1)} %copy-done.12), channel_id=1, source_target_pairs={{16,0},{32,16},{48,32},{64,48},{80,64},{96,80},{112,96},{128,112},... | collective-permute-start | bytes 786440 | tf_op jit(solution)/shard_map/while/body/eval_jaxpr/ppermute | solution.py:13
  231.5 7.9 %collective-permute-start.1 = (bf16[1,32,32,128]{3,2,1,0:T(8,128)(2,1)}, bf16[1,32,32,128]{3,2,1,0:T(8,128)(2,1)S(1)}, u32[]{:S(2)}, u32[]{:S(2)}) collective-permute-start(bf16[1,32,32,128]{3,2,1,0:T(8,128)(2,1)} %copy-done.12), channel_id=1, source_target_pairs={{16,0},{32,16},{48,32},{64,48},{80,64},{96,80},{112,96},{128,112},... | collective-permute-start | bytes 786440 | tf_op jit(solution)/shard_map/while/body/eval_jaxpr/ppermute | solution.py:13
  240.3 8.4 %collective-permute-start.1 = (bf16[1,32,32,128]{3,2,1,0:T(8,128)(2,1)}, bf16[1,32,32,128]{3,2,1,0:T(8,128)(2,1)S(1)}, u32[]{:S(2)}, u32[]{:S(2)}) collective-permute-start(bf16[1,32,32,128]{3,2,1,0:T(8,128)(2,1)} %copy-done.12), channel_id=1, source_target_pairs={{16,0},{32,16},{48,32},{64,48},{80,64},{96,80},{112,96},{128,112},... | collective-permute-start | bytes 786440 | tf_op jit(solution)/shard_map/while/body/eval_jaxpr/ppermute | solution.py:13
  249.6 9.8 %collective-permute-start.1 = (bf16[1,32,32,128]{3,2,1,0:T(8,128)(2,1)}, bf16[1,32,32,128]{3,2,1,0:T(8,128)(2,1)S(1)}, u32[]{:S(2)}, u32[]{:S(2)}) collective-permute-start(bf16[1,32,32,128]{3,2,1,0:T(8,128)(2,1)} %copy-done.12), channel_id=1, source_target_pairs={{16,0},{32,16},{48,32},{64,48},{80,64},{96,80},{112,96},{128,112},... | collective-permute-start | bytes 786440 | tf_op jit(solution)/shard_map/while/body/eval_jaxpr/ppermute | solution.py:13
  260.3 11.4 %collective-permute-start.1 = (bf16[1,32,32,128]{3,2,1,0:T(8,128)(2,1)}, bf16[1,32,32,128]{3,2,1,0:T(8,128)(2,1)S(1)}, u32[]{:S(2)}, u32[]{:S(2)}) collective-permute-start(bf16[1,32,32,128]{3,2,1,0:T(8,128)(2,1)} %copy-done.12), channel_id=1, source_target_pairs={{16,0},{32,16},{48,32},{64,48},{80,64},{96,80},{112,96},{128,112},... | collective-permute-start | bytes 786440 | tf_op jit(solution)/shard_map/while/body/eval_jaxpr/ppermute | solution.py:13
  272.6 9.7 %collective-permute-start.1 = (bf16[1,32,32,128]{3,2,1,0:T(8,128)(2,1)}, bf16[1,32,32,128]{3,2,1,0:T(8,128)(2,1)S(1)}, u32[]{:S(2)}, u32[]{:S(2)}) collective-permute-start(bf16[1,32,32,128]{3,2,1,0:T(8,128)(2,1)} %copy-done.12), channel_id=1, source_target_pairs={{16,0},{32,16},{48,32},{64,48},{80,64},{96,80},{112,96},{128,112},... | collective-permute-start | bytes 786440 | tf_op jit(solution)/shard_map/while/body/eval_jaxpr/ppermute | solution.py:13
  283.3 9.1 %collective-permute-start.1 = (bf16[1,32,32,128]{3,2,1,0:T(8,128)(2,1)}, bf16[1,32,32,128]{3,2,1,0:T(8,128)(2,1)S(1)}, u32[]{:S(2)}, u32[]{:S(2)}) collective-permute-start(bf16[1,32,32,128]{3,2,1,0:T(8,128)(2,1)} %copy-done.12), channel_id=1, source_target_pairs={{16,0},{32,16},{48,32},{64,48},{80,64},{96,80},{112,96},{128,112},... | collective-permute-start | bytes 786440 | tf_op jit(solution)/shard_map/while/body/eval_jaxpr/ppermute | solution.py:13
  293.3 9.1 %collective-permute-start.1 = (bf16[1,32,32,128]{3,2,1,0:T(8,128)(2,1)}, bf16[1,32,32,128]{3,2,1,0:T(8,128)(2,1)S(1)}, u32[]{:S(2)}, u32[]{:S(2)}) collective-permute-start(bf16[1,32,32,128]{3,2,1,0:T(8,128)(2,1)} %copy-done.12), channel_id=1, source_target_pairs={{16,0},{32,16},{48,32},{64,48},{80,64},{96,80},{112,96},{128,112},... | collective-permute-start | bytes 786440 | tf_op jit(solution)/shard_map/while/body/eval_jaxpr/ppermute | solution.py:13
  303.4 9.1 %collective-permute-start.1 = (bf16[1,32,32,128]{3,2,1,0:T(8,128)(2,1)}, bf16[1,32,32,128]{3,2,1,0:T(8,128)(2,1)S(1)}, u32[]{:S(2)}, u32[]{:S(2)}) collective-permute-start(bf16[1,32,32,128]{3,2,1,0:T(8,128)(2,1)} %copy-done.12), channel_id=1, source_target_pairs={{16,0},{32,16},{48,32},{64,48},{80,64},{96,80},{112,96},{128,112},... | collective-permute-start | bytes 786440 | tf_op jit(solution)/shard_map/while/body/eval_jaxpr/ppermute | solution.py:13
  313.4 9.1 %collective-permute-start.1 = (bf16[1,32,32,128]{3,2,1,0:T(8,128)(2,1)}, bf16[1,32,32,128]{3,2,1,0:T(8,128)(2,1)S(1)}, u32[]{:S(2)}, u32[]{:S(2)}) collective-permute-start(bf16[1,32,32,128]{3,2,1,0:T(8,128)(2,1)} %copy-done.12), channel_id=1, source_target_pairs={{16,0},{32,16},{48,32},{64,48},{80,64},{96,80},{112,96},{128,112},... | collective-permute-start | bytes 786440 | tf_op jit(solution)/shard_map/while/body/eval_jaxpr/ppermute | solution.py:13
  323.4 9.1 %collective-permute-start.1 = (bf16[1,32,32,128]{3,2,1,0:T(8,128)(2,1)}, bf16[1,32,32,128]{3,2,1,0:T(8,128)(2,1)S(1)}, u32[]{:S(2)}, u32[]{:S(2)}) collective-permute-start(bf16[1,32,32,128]{3,2,1,0:T(8,128)(2,1)} %copy-done.12), channel_id=1, source_target_pairs={{16,0},{32,16},{48,32},{64,48},{80,64},{96,80},{112,96},{128,112},... | collective-permute-start | bytes 786440 | tf_op jit(solution)/shard_map/while/body/eval_jaxpr/ppermute | solution.py:13
  333.5 9.1 %collective-permute-start.1 = (bf16[1,32,32,128]{3,2,1,0:T(8,128)(2,1)}, bf16[1,32,32,128]{3,2,1,0:T(8,128)(2,1)S(1)}, u32[]{:S(2)}, u32[]{:S(2)}) collective-permute-start(bf16[1,32,32,128]{3,2,1,0:T(8,128)(2,1)} %copy-done.12), channel_id=1, source_target_pairs={{16,0},{32,16},{48,32},{64,48},{80,64},{96,80},{112,96},{128,112},... | collective-permute-start | bytes 786440 | tf_op jit(solution)/shard_map/while/body/eval_jaxpr/ppermute | solution.py:13
  343.5 25.8 %collective-permute-start.1 = (bf16[1,32,32,128]{3,2,1,0:T(8,128)(2,1)}, bf16[1,32,32,128]{3,2,1,0:T(8,128)(2,1)S(1)}, u32[]{:S(2)}, u32[]{:S(2)}) collective-permute-start(bf16[1,32,32,128]{3,2,1,0:T(8,128)(2,1)} %copy-done.12), channel_id=1, source_target_pairs={{16,0},{32,16},{48,32},{64,48},{80,64},{96,80},{112,96},{128,112},... | collective-permute-start | bytes 786440 | tf_op jit(solution)/shard_map/while/body/eval_jaxpr/ppermute | solution.py:13
  373.5 6.1 %collective-permute-start.1 = (bf16[1,32,32,128]{3,2,1,0:T(8,128)(2,1)}, bf16[1,32,32,128]{3,2,1,0:T(8,128)(2,1)S(1)}, u32[]{:S(2)}, u32[]{:S(2)}) collective-permute-start(bf16[1,32,32,128]{3,2,1,0:T(8,128)(2,1)} %copy-done.12), channel_id=1, source_target_pairs={{16,0},{32,16},{48,32},{64,48},{80,64},{96,80},{112,96},{128,112},... | collective-permute-start | bytes 786440 | tf_op jit(solution)/shard_map/while/body/eval_jaxpr/ppermute | solution.py:13
  380.6 11.2 %collective-permute-start.1 = (bf16[1,32,32,128]{3,2,1,0:T(8,128)(2,1)}, bf16[1,32,32,128]{3,2,1,0:T(8,128)(2,1)S(1)}, u32[]{:S(2)}, u32[]{:S(2)}) collective-permute-start(bf16[1,32,32,128]{3,2,1,0:T(8,128)(2,1)} %copy-done.12), channel_id=1, source_target_pairs={{16,0},{32,16},{48,32},{64,48},{80,64},{96,80},{112,96},{128,112},... | collective-permute-start | bytes 786440 | tf_op jit(solution)/shard_map/while/body/eval_jaxpr/ppermute | solution.py:13
  395.3 1.3 copy-start.14
  401.0 1.2 copy-start.22
  458.9 2.0 copy-start.30
  459.7 1.5 copy-start.28
  (44 other events, 36.4 us)
Sparse Core Ops, SparseCore 0:
  416.7 101.0 all-reduce.19
where the time goes:
time: 529 us; the launch traced here: 528 us
  waiting for transfers between devices  297 us (56%)
  starting transfers between devices  67.2 us (13%)
  matrix products  47.4 us (9%)
  blocking collectives  40.9 us (8%)
  local copies, waits for them, and re-layouts  40.5 us (8%)
  between operations  15.9 us (3%)
  other arithmetic  15.6 us (3%)
    ppermute x30, waiting for transfers between devices, passed_along(): return lax.ppermute(x, axis, pairs)  244 us
    ppermute x30, starting transfers between devices, passed_along(): return lax.ppermute(x, axis, pairs)  67.2 us
    psum x1, waiting for transfers between devices, local(): lax.psum(kernel_stack.astype(jnp.bfloat16), 'dp').astype(jnp.float32)  53.4 us
    psum x1, blocking collectives, local(): lax.psum(bias_stack.astype(jnp.bfloat16), 'dp').astype(jnp.float32)  40.9 us
    while x60, local copies, waits for them, and re-layouts  22.5 us
    dot_general x81, matrix products, transposed(): lax.dot_general(view, kernel[tap_index], (((1,), (1,)), ((), ())), prefer...  19.6 us
    dot_general x81, matrix products, convolve(): jnp.dot(view, kernel[tap_index], preferred_element_type=jnp.float32)  18.1 us
  transfers between devices with their start and end apart: 31, of which 31 were waited for; matrix products, arithmetic and copies ran while one was open for 1% of the time, Pallas kernels for 0%

commit v1 on v0

--- a/solution.py
+++ b/solution.py
@@ -147,7 +147,9 @@
     kernel_stack = jnp.stack(kernel_grads)
     bias_stack = jnp.stack(bias_grads)
     kernel_stack, bias_stack = (
-        lax.psum(kernel_stack.astype(jnp.bfloat16), "dp").astype(jnp.float32),
+        jnp.sum(lax.all_gather(kernel_stack.astype(jnp.bfloat16), "dp"), axis=0).astype(
+            jnp.float32
+        ),
         lax.psum(bias_stack.astype(jnp.bfloat16), "dp").astype(jnp.float32),
     )
     return (current_state[None], adjoint[None], kernel_stack, bias_stack)

time: 529 us -> 577 us (1.091); the launches traced: 528 us -> 568 us
  waiting for transfers between devices: 297 us -> 329 us
  other arithmetic: 15.6 us -> 28.4 us
    all_gather x0 -> x1, waiting for transfers between devices: none -> 85 us  [local(): lax.all_gather(kernel_stack.astype(jnp.bfloat16), 'dp')]
    psum x1 -> x0, waiting for transfers between devices: 53.4 us -> none  [local(): lax.psum(kernel_stack.astype(jnp.bfloat16), 'dp').astype(jnp.float32)]
    while x60 -> x30, local copies, waits for them, and re-layouts: 22.5 us -> 10.8 us
    another operation x28, local copies, waits for them, and re-layouts: 1.22 us -> 12.5 us
    reduce_sum x0 -> x1, other arithmetic: none -> 10.6 us  [local(): jnp.sum(lax.all_gather(kernel_stack.astype(jnp.bfloat16), 'dp'), axis=0)]
where the time goes in v1:
time: 577 us; the launch traced here: 568 us
  waiting for transfers between devices  329 us (57%)
  starting transfers between devices  68.5 us (12%)
  matrix products  46.1 us (8%)
  blocking collectives  41.7 us (7%)
  local copies, waits for them, and re-layouts  35.5 us (6%)
  other arithmetic  28.4 us (5%)
  between operations  16.2 us (3%)
    ppermute x30, waiting for transfers between devices, passed_along(): return lax.ppermute(x, axis, pairs)  245 us
    all_gather x1, waiting for transfers between devices, local(): lax.all_gather(kernel_stack.astype(jnp.bfloat16), 'dp')  85 us
    ppermute x30, starting transfers between devices, passed_along(): return lax.ppermute(x, axis, pairs)  68.4 us
    psum x1, blocking collectives, local(): lax.psum(bias_stack.astype(jnp.bfloat16), 'dp').astype(jnp.float32)  41.7 us
    dot_general x81, matrix products, transposed(): lax.dot_general(view, kernel[tap_index], (((1,), (1,)), ((), ())), prefer...  19.3 us
    dot_general x81, matrix products, convolve(): jnp.dot(view, kernel[tap_index], preferred_element_type=jnp.float32)  17.1 us
    another operation x28, local copies, waits for them, and re-layouts  12.5 us
  transfers between devices with their start and end apart: 31, of which 31 were waited for; matrix products, arithmetic and copies ran while one was open for 1% of the time, Pallas kernels for 0%

profile of v1, /device:TPU:32, one launch (start us, length us, event | category | flops | bytes accessed | tf_op | source)
XLA Modules:
  0.0 568.3 jit_solution(1352954768719179598)
XLA Ops:
  20.1 183.3 %while.30 = (s32[]{:T(128)}, f32[1,32,32,128]{3,2,1,0:T(8,128)S(1)}, s32[]{:T(128)}, bf16[9,128,128]{2,1,0:T(8,128)(2,1)S(1)}, bf16[128]{0:T(256)(128)(2,1)S(1)}, /*index=5*/f32[1,32,32,128]{3,2,1,0:T(8,128)}, s32[]{:T(128)}) while((s32[]{:T(128)}, f32[1,32,32,128]{3,2,1,0:T(8,128)S(1)}, s32[]{:T(128)}, bf16[9,128,128]{2,1,0:T(8,128)(2,1)S(1)}, ...), condition=%wide.region_3.4_spmd, body=%wide.region_0.3_spmd.sunk | while | flops 303693952 | bytes 22578640 | solution.py:105
  21.0 1.9 collective-permute-start
  22.9 8.9 %collective-permute-done = f32[1,32,32,128]{3,2,1,0:T(8,128)} collective-permute-done((f32[1,32,32,128]{3,2,1,0:T(8,128)}, f32[1,32,32,128]{3,2,1,0:T(8,128)}, u32[]{:S(2)}, u32[]{:S(2)}) %collective-permute-start) | collective-permute-done | bytes 524320 | tf_op jit(solution)/shard_map/while/body/eval_jaxpr/ppermute | solution.py:13
  32.8 1.9 collective-permute-start
  34.7 10.5 %collective-permute-done = f32[1,32,32,128]{3,2,1,0:T(8,128)} collective-permute-done((f32[1,32,32,128]{3,2,1,0:T(8,128)}, f32[1,32,32,128]{3,2,1,0:T(8,128)}, u32[]{:S(2)}, u32[]{:S(2)}) %collective-permute-start) | collective-permute-done | bytes 524320 | tf_op jit(solution)/shard_map/while/body/eval_jaxpr/ppermute | solution.py:13
  46.4 3.9 conditional.4
  50.3 1.9 collective-permute-start
  52.3 8.9 %collective-permute-done = f32[1,32,32,128]{3,2,1,0:T(8,128)} collective-permute-done((f32[1,32,32,128]{3,2,1,0:T(8,128)}, f32[1,32,32,128]{3,2,1,0:T(8,128)}, u32[]{:S(2)}, u32[]{:S(2)}) %collective-permute-start) | collective-permute-done | bytes 524320 | tf_op jit(solution)/shard_map/while/body/eval_jaxpr/ppermute | solution.py:13
  62.2 1.9 collective-permute-start
  64.1 8.9 %collective-permute-done = f32[1,32,32,128]{3,2,1,0:T(8,128)} collective-permute-done((f32[1,32,32,128]{3,2,1,0:T(8,128)}, f32[1,32,32,128]{3,2,1,0:T(8,128)}, u32[]{:S(2)}, u32[]{:S(2)}) %collective-permute-start) | collective-permute-done | bytes 524320 | tf_op jit(solution)/shard_map/while/body/eval_jaxpr/ppermute | solution.py:13
  74.0 1.9 collective-permute-start
  75.9 8.9 %collective-permute-done = f32[1,32,32,128]{3,2,1,0:T(8,128)} collective-permute-done((f32[1,32,32,128]{3,2,1,0:T(8,128)}, f32[1,32,32,128]{3,2,1,0:T(8,128)}, u32[]{:S(2)}, u32[]{:S(2)}) %collective-permute-start) | collective-permute-done | bytes 524320 | tf_op jit(solution)/shard_map/while/body/eval_jaxpr/ppermute | solution.py:13
  85.8 1.9 collective-permute-start
  87.7 8.9 %collective-permute-done = f32[1,32,32,128]{3,2,1,0:T(8,128)} collective-permute-done((f32[1,32,32,128]{3,2,1,0:T(8,128)}, f32[1,32,32,128]{3,2,1,0:T(8,128)}, u32[]{:S(2)}, u32[]{:S(2)}) %collective-permute-start) | collective-permute-done | bytes 524320 | tf_op jit(solution)/shard_map/while/body/eval_jaxpr/ppermute | solution.py:13
  99.6 8.9 %collective-permute-done = f32[1,32,32,128]{3,2,1,0:T(8,128)} collective-permute-done((f32[1,32,32,128]{3,2,1,0:T(8,128)}, f32[1,32,32,128]{3,2,1,0:T(8,128)}, u32[]{:S(2)}, u32[]{:S(2)}) %collective-permute-start) | collective-permute-done | bytes 524320 | tf_op jit(solution)/shard_map/while/body/eval_jaxpr/ppermute | solution.py:13
  111.4 8.9 %collective-permute-done = f32[1,32,32,128]{3,2,1,0:T(8,128)} collective-permute-done((f32[1,32,32,128]{3,2,1,0:T(8,128)}, f32[1,32,32,128]{3,2,1,0:T(8,128)}, u32[]{:S(2)}, u32[]{:S(2)}) %collective-permute-start) | collective-permute-done | bytes 524320 | tf_op jit(solution)/shard_map/while/body/eval_jaxpr/ppermute | solution.py:13
  123.2 8.9 %collective-permute-done = f32[1,32,32,128]{3,2,1,0:T(8,128)} collective-permute-done((f32[1,32,32,128]{3,2,1,0:T(8,128)}, f32[1,32,32,128]{3,2,1,0:T(8,128)}, u32[]{:S(2)}, u32[]{:S(2)}) %collective-permute-start) | collective-permute-done | bytes 524320 | tf_op jit(solution)/shard_map/while/body/eval_jaxpr/ppermute | solution.py:13
  135.1 8.9 %collective-permute-done = f32[1,32,32,128]{3,2,1,0:T(8,128)} collective-permute-done((f32[1,32,32,128]{3,2,1,0:T(8,128)}, f32[1,32,32,128]{3,2,1,0:T(8,128)}, u32[]{:S(2)}, u32[]{:S(2)}) %collective-permute-start) | collective-permute-done | bytes 524320 | tf_op jit(solution)/shard_map/while/body/eval_jaxpr/ppermute | solution.py:13
  146.9 8.9 %collective-permute-done = f32[1,32,32,128]{3,2,1,0:T(8,128)} collective-permute-done((f32[1,32,32,128]{3,2,1,0:T(8,128)}, f32[1,32,32,128]{3,2,1,0:T(8,128)}, u32[]{:S(2)}, u32[]{:S(2)}) %collective-permute-start) | collective-permute-done | bytes 524320 | tf_op jit(solution)/shard_map/while/body/eval_jaxpr/ppermute | solution.py:13
  158.7 8.9 %collective-permute-done = f32[1,32,32,128]{3,2,1,0:T(8,128)} collective-permute-done((f32[1,32,32,128]{3,2,1,0:T(8,128)}, f32[1,32,32,128]{3,2,1,0:T(8,128)}, u32[]{:S(2)}, u32[]{:S(2)}) %collective-permute-start) | collective-permute-done | bytes 524320 | tf_op jit(solution)/shard_map/while/body/eval_jaxpr/ppermute | solution.py:13
  170.6 8.9 %collective-permute-done = f32[1,32,32,128]{3,2,1,0:T(8,128)} collective-permute-done((f32[1,32,32,128]{3,2,1,0:T(8,128)}, f32[1,32,32,128]{3,2,1,0:T(8,128)}, u32[]{:S(2)}, u32[]{:S(2)}) %collective-permute-start) | collective-permute-done | bytes 524320 | tf_op jit(solution)/shard_map/while/body/eval_jaxpr/ppermute | solution.py:13
  182.4 8.9 %collective-permute-done = f32[1,32,32,128]{3,2,1,0:T(8,128)} collective-permute-done((f32[1,32,32,128]{3,2,1,0:T(8,128)}, f32[1,32,32,128]{3,2,1,0:T(8,128)}, u32[]{:S(2)}, u32[]{:S(2)}) %collective-permute-start) | collective-permute-done | bytes 524320 | tf_op jit(solution)/shard_map/while/body/eval_jaxpr/ppermute | solution.py:13
  194.2 8.9 %collective-permute-done = f32[1,32,32,128]{3,2,1,0:T(8,128)} collective-permute-done((f32[1,32,32,128]{3,2,1,0:T(8,128)}, f32[1,32,32,128]{3,2,1,0:T(8,128)}, u32[]{:S(2)}, u32[]{:S(2)}) %collective-permute-start) | collective-permute-done | bytes 524320 | tf_op jit(solution)/shard_map/while/body/eval_jaxpr/ppermute | solution.py:13
  225.6 167.3 %while.31 = (s32[]{:T(128)}, f32[1,32,32,128]{3,2,1,0:T(8,128)S(1)}, s32[]{:T(128)}, f32[1,32,32,128]{3,2,1,0:T(8,128)S(1)}, f32[1,32,32,128]{3,2,1,0:T(8,128)S(...) while((s32[]{:T(128)}, ...), condition=%wide.region_7.8_spmd, body=%wide.region_4.7_spmd.sunk | while | flops 304087040 | bytes 23626028 | solution.py:136
  228.5 4.2 collective-permute-done.1
  233.6 3.7 collective-permute-start.1
  237.3 4.2 collective-permute-done.1
  242.4 3.7 collective-permute-start.1
  246.1 4.2 collective-permute-done.1
  251.2 3.7 collective-permute-start.1
  255.0 5.3 collective-permute-done.1
  261.2 2.6 collective-permute-start.1
  263.8 8.7 %collective-permute-done.1 = bf16[1,32,32,128]{3,2,1,0:T(8,128)(2,1)S(1)} collective-permute-done((bf16[1,32,32,128]{3,2,1,0:T(8,128)(2,1)}, bf16[1,32,32,128]{3,2,1,0:T(8,128)(2,1)S(1)}, u32[]{:S(2)}, u32[]{:S(2)}) %collective-permute-start.1) | collective-permute-done | bytes 262176 | tf_op jit(solution)/shard_map/while/body/eval_jaxpr/ppermute | solution.py:13
  275.4 7.9 %collective-permute-done.1 = bf16[1,32,32,128]{3,2,1,0:T(8,128)(2,1)S(1)} collective-permute-done((bf16[1,32,32,128]{3,2,1,0:T(8,128)(2,1)}, bf16[1,32,32,128]{3,2,1,0:T(8,128)(2,1)S(1)}, u32[]{:S(2)}, u32[]{:S(2)}) %collective-permute-start.1) | collective-permute-done | bytes 262176 | tf_op jit(solution)/shard_map/while/body/eval_jaxpr/ppermute | solution.py:13
  286.2 7.2 %collective-permute-done.1 = bf16[1,32,32,128]{3,2,1,0:T(8,128)(2,1)S(1)} collective-permute-done((bf16[1,32,32,128]{3,2,1,0:T(8,128)(2,1)}, bf16[1,32,32,128]{3,2,1,0:T(8,128)(2,1)S(1)}, u32[]{:S(2)}, u32[]{:S(2)}) %collective-permute-start.1) | collective-permute-done | bytes 262176 | tf_op jit(solution)/shard_map/while/body/eval_jaxpr/ppermute | solution.py:13
  296.2 7.2 %collective-permute-done.1 = bf16[1,32,32,128]{3,2,1,0:T(8,128)(2,1)S(1)} collective-permute-done((bf16[1,32,32,128]{3,2,1,0:T(8,128)(2,1)}, bf16[1,32,32,128]{3,2,1,0:T(8,128)(2,1)S(1)}, u32[]{:S(2)}, u32[]{:S(2)}) %collective-permute-start.1) | collective-permute-done | bytes 262176 | tf_op jit(solution)/shard_map/while/body/eval_jaxpr/ppermute | solution.py:13
  306.2 7.2 %collective-permute-done.1 = bf16[1,32,32,128]{3,2,1,0:T(8,128)(2,1)S(1)} collective-permute-done((bf16[1,32,32,128]{3,2,1,0:T(8,128)(2,1)}, bf16[1,32,32,128]{3,2,1,0:T(8,128)(2,1)S(1)}, u32[]{:S(2)}, u32[]{:S(2)}) %collective-permute-start.1) | collective-permute-done | bytes 262176 | tf_op jit(solution)/shard_map/while/body/eval_jaxpr/ppermute | solution.py:13
  316.3 7.2 %collective-permute-done.1 = bf16[1,32,32,128]{3,2,1,0:T(8,128)(2,1)S(1)} collective-permute-done((bf16[1,32,32,128]{3,2,1,0:T(8,128)(2,1)}, bf16[1,32,32,128]{3,2,1,0:T(8,128)(2,1)S(1)}, u32[]{:S(2)}, u32[]{:S(2)}) %collective-permute-start.1) | collective-permute-done | bytes 262176 | tf_op jit(solution)/shard_map/while/body/eval_jaxpr/ppermute | solution.py:13
  326.3 7.2 %collective-permute-done.1 = bf16[1,32,32,128]{3,2,1,0:T(8,128)(2,1)S(1)} collective-permute-done((bf16[1,32,32,128]{3,2,1,0:T(8,128)(2,1)}, bf16[1,32,32,128]{3,2,1,0:T(8,128)(2,1)S(1)}, u32[]{:S(2)}, u32[]{:S(2)}) %collective-permute-start.1) | collective-permute-done | bytes 262176 | tf_op jit(solution)/shard_map/while/body/eval_jaxpr/ppermute | solution.py:13
  336.4 7.2 %collective-permute-done.1 = bf16[1,32,32,128]{3,2,1,0:T(8,128)(2,1)S(1)} collective-permute-done((bf16[1,32,32,128]{3,2,1,0:T(8,128)(2,1)}, bf16[1,32,32,128]{3,2,1,0:T(8,128)(2,1)S(1)}, u32[]{:S(2)}, u32[]{:S(2)}) %collective-permute-start.1) | collective-permute-done | bytes 262176 | tf_op jit(solution)/shard_map/while/body/eval_jaxpr/ppermute | solution.py:13
  346.4 23.9 %collective-permute-done.1 = bf16[1,32,32,128]{3,2,1,0:T(8,128)(2,1)S(1)} collective-permute-done((bf16[1,32,32,128]{3,2,1,0:T(8,128)(2,1)}, bf16[1,32,32,128]{3,2,1,0:T(8,128)(2,1)S(1)}, u32[]{:S(2)}, u32[]{:S(2)}) %collective-permute-start.1) | collective-permute-done | bytes 262176 | tf_op jit(solution)/shard_map/while/body/eval_jaxpr/ppermute | solution.py:13
  370.4 3.3 conditional.5
  376.4 4.2 collective-permute-done.1
  381.5 7.0 %collective-permute-start.1 = (bf16[1,32,32,128]{3,2,1,0:T(8,128)(2,1)}, bf16[1,32,32,128]{3,2,1,0:T(8,128)(2,1)S(1)}, u32[]{:S(2)}, u32[]{:S(2)}) collective-permute-start(bf16[1,32,32,128]{3,2,1,0:T(8,128)(2,1)} %copy-done.10), channel_id=1, source_target_pairs={{16,0},{32,16},{48,32},{64,48},{80,64},{96,80},{112,96},{128,112},... | collective-permute-start | bytes 786440 | tf_op jit(solution)/shard_map/while/body/eval_jaxpr/ppermute | solution.py:13
  388.5 4.2 collective-permute-done.1
  417.7 41.7 %psum.7 = bf16[4,128]{1,0:T(4,128)(2,1)S(1)} all-reduce(bf16[4,128]{1,0:T(4,128)(2,1)S(1)} %pad_maximum_fusion.1), channel_id=1, replica_groups=mesh['layer'=16,'dp'=16] {'dp'}, use_global_device_ids=true, to_apply=%region_13.14 | all-reduce | flops 512 | bytes 2048 | tf_op jit(solution)/shard_map/psum | solution.py:153
  463.9 85.0 %all-gather.2.cloned.1.call-done = bf16[16,4,9,128,128]{4,3,2,1,0:T(8,128)(2,1)} async-done(((bf16[1,4,9,128,128]{4,3,2,1,0:T(8,128)(2,1)}), bf16[16,4,9,128,128]{4,3,2,1,0:T(8,128)(2,1)}) %all-gather.2.cloned.1.call-update) | async-done | bytes 18874384 | tf_op jit(solution)/shard_map/all_gather | solution.py:150
  548.8 10.6 %reduce_sum.48 = bf16[4,9,128,128]{3,2,1,0:T(8,128)(2,1)S(1)} reduce(bf16[16,4,9,128,128]{4,3,2,1,0:T(8,128)(2,1)} %all-gather.2.cloned.1.call-done, bf16[]{:T(256)} %constant.73.clone.1), dimensions={0}, to_apply=%region_8.9 | reduce | flops 8847360 | bytes 20054018 | tf_op jit(solution)/shard_map/reduce_sum | solution.py:150
  (430 shorter events, 148.7 us)
Async XLA Ops:
  7.2 2.1 copy-start
  7.2 2.1 copy-start.1
  7.2 541.7 %all-gather.2.cloned.1.call-start = ((), (), s32[]{:S(2)}) async-start(), calls=%async_computation | async-start | bytes 20054016 | tf_op jit(solution)/shard_map/all_gather | solution.py:150
  21.0 10.8 %collective-permute-start = (f32[1,32,32,128]{3,2,1,0:T(8,128)}, f32[1,32,32,128]{3,2,1,0:T(8,128)}, u32[]{:S(2)}, u32[]{:S(2)}) collective-permute-start(f32[1,32,32,128]{3,2,1,0:T(8,128)} %get-tuple-element.735), channel_id=1, source_target_pairs={{0,16},{16,32},{32,48},{48,64},{64,80},{80,96},{96,112},{112,128},... | collective-permute-start | bytes 1572872 | tf_op jit(solution)/shard_map/while/body/eval_jaxpr/ppermute | solution.py:13
  32.8 12.4 %collective-permute-start = (f32[1,32,32,128]{3,2,1,0:T(8,128)}, f32[1,32,32,128]{3,2,1,0:T(8,128)}, u32[]{:S(2)}, u32[]{:S(2)}) collective-permute-start(f32[1,32,32,128]{3,2,1,0:T(8,128)} %get-tuple-element.735), channel_id=1, source_target_pairs={{0,16},{16,32},{32,48},{48,64},{64,80},{80,96},{96,112},{112,128},... | collective-permute-start | bytes 1572872 | tf_op jit(solution)/shard_map/while/body/eval_jaxpr/ppermute | solution.py:13
  48.3 1.0 copy-start.3
  50.3 10.8 %collective-permute-start = (f32[1,32,32,128]{3,2,1,0:T(8,128)}, f32[1,32,32,128]{3,2,1,0:T(8,128)}, u32[]{:S(2)}, u32[]{:S(2)}) collective-permute-start(f32[1,32,32,128]{3,2,1,0:T(8,128)} %get-tuple-element.735), channel_id=1, source_target_pairs={{0,16},{16,32},{32,48},{48,64},{64,80},{80,96},{96,112},{112,128},... | collective-permute-start | bytes 1572872 | tf_op jit(solution)/shard_map/while/body/eval_jaxpr/ppermute | solution.py:13
  62.2 10.8 %collective-permute-start = (f32[1,32,32,128]{3,2,1,0:T(8,128)}, f32[1,32,32,128]{3,2,1,0:T(8,128)}, u32[]{:S(2)}, u32[]{:S(2)}) collective-permute-start(f32[1,32,32,128]{3,2,1,0:T(8,128)} %get-tuple-element.735), channel_id=1, source_target_pairs={{0,16},{16,32},{32,48},{48,64},{64,80},{80,96},{96,112},{112,128},... | collective-permute-start | bytes 1572872 | tf_op jit(solution)/shard_map/while/body/eval_jaxpr/ppermute | solution.py:13
  74.0 10.8 %collective-permute-start = (f32[1,32,32,128]{3,2,1,0:T(8,128)}, f32[1,32,32,128]{3,2,1,0:T(8,128)}, u32[]{:S(2)}, u32[]{:S(2)}) collective-permute-start(f32[1,32,32,128]{3,2,1,0:T(8,128)} %get-tuple-element.735), channel_id=1, source_target_pairs={{0,16},{16,32},{32,48},{48,64},{64,80},{80,96},{96,112},{112,128},... | collective-permute-start | bytes 1572872 | tf_op jit(solution)/shard_map/while/body/eval_jaxpr/ppermute | solution.py:13
  85.8 10.8 %collective-permute-start = (f32[1,32,32,128]{3,2,1,0:T(8,128)}, f32[1,32,32,128]{3,2,1,0:T(8,128)}, u32[]{:S(2)}, u32[]{:S(2)}) collective-permute-start(f32[1,32,32,128]{3,2,1,0:T(8,128)} %get-tuple-element.735), channel_id=1, source_target_pairs={{0,16},{16,32},{32,48},{48,64},{64,80},{80,96},{96,112},{112,128},... | collective-permute-start | bytes 1572872 | tf_op jit(solution)/shard_map/while/body/eval_jaxpr/ppermute | solution.py:13
  97.7 10.8 %collective-permute-start = (f32[1,32,32,128]{3,2,1,0:T(8,128)}, f32[1,32,32,128]{3,2,1,0:T(8,128)}, u32[]{:S(2)}, u32[]{:S(2)}) collective-permute-start(f32[1,32,32,128]{3,2,1,0:T(8,128)} %get-tuple-element.735), channel_id=1, source_target_pairs={{0,16},{16,32},{32,48},{48,64},{64,80},{80,96},{96,112},{112,128},... | collective-permute-start | bytes 1572872 | tf_op jit(solution)/shard_map/while/body/eval_jaxpr/ppermute | solution.py:13
  109.5 10.8 %collective-permute-start = (f32[1,32,32,128]{3,2,1,0:T(8,128)}, f32[1,32,32,128]{3,2,1,0:T(8,128)}, u32[]{:S(2)}, u32[]{:S(2)}) collective-permute-start(f32[1,32,32,128]{3,2,1,0:T(8,128)} %get-tuple-element.735), channel_id=1, source_target_pairs={{0,16},{16,32},{32,48},{48,64},{64,80},{80,96},{96,112},{112,128},... | collective-permute-start | bytes 1572872 | tf_op jit(solution)/shard_map/while/body/eval_jaxpr/ppermute | solution.py:13
  121.3 10.8 %collective-permute-start = (f32[1,32,32,128]{3,2,1,0:T(8,128)}, f32[1,32,32,128]{3,2,1,0:T(8,128)}, u32[]{:S(2)}, u32[]{:S(2)}) collective-permute-start(f32[1,32,32,128]{3,2,1,0:T(8,128)} %get-tuple-element.735), channel_id=1, source_target_pairs={{0,16},{16,32},{32,48},{48,64},{64,80},{80,96},{96,112},{112,128},... | collective-permute-start | bytes 1572872 | tf_op jit(solution)/shard_map/while/body/eval_jaxpr/ppermute | solution.py:13
  133.2 10.8 %collective-permute-start = (f32[1,32,32,128]{3,2,1,0:T(8,128)}, f32[1,32,32,128]{3,2,1,0:T(8,128)}, u32[]{:S(2)}, u32[]{:S(2)}) collective-permute-start(f32[1,32,32,128]{3,2,1,0:T(8,128)} %get-tuple-element.735), channel_id=1, source_target_pairs={{0,16},{16,32},{32,48},{48,64},{64,80},{80,96},{96,112},{112,128},... | collective-permute-start | bytes 1572872 | tf_op jit(solution)/shard_map/while/body/eval_jaxpr/ppermute | solution.py:13
  145.0 10.8 %collective-permute-start = (f32[1,32,32,128]{3,2,1,0:T(8,128)}, f32[1,32,32,128]{3,2,1,0:T(8,128)}, u32[]{:S(2)}, u32[]{:S(2)}) collective-permute-start(f32[1,32,32,128]{3,2,1,0:T(8,128)} %get-tuple-element.735), channel_id=1, source_target_pairs={{0,16},{16,32},{32,48},{48,64},{64,80},{80,96},{96,112},{112,128},... | collective-permute-start | bytes 1572872 | tf_op jit(solution)/shard_map/while/body/eval_jaxpr/ppermute | solution.py:13
  156.8 10.8 %collective-permute-start = (f32[1,32,32,128]{3,2,1,0:T(8,128)}, f32[1,32,32,128]{3,2,1,0:T(8,128)}, u32[]{:S(2)}, u32[]{:S(2)}) collective-permute-start(f32[1,32,32,128]{3,2,1,0:T(8,128)} %get-tuple-element.735), channel_id=1, source_target_pairs={{0,16},{16,32},{32,48},{48,64},{64,80},{80,96},{96,112},{112,128},... | collective-permute-start | bytes 1572872 | tf_op jit(solution)/shard_map/while/body/eval_jaxpr/ppermute | solution.py:13
  168.6 10.8 %collective-permute-start = (f32[1,32,32,128]{3,2,1,0:T(8,128)}, f32[1,32,32,128]{3,2,1,0:T(8,128)}, u32[]{:S(2)}, u32[]{:S(2)}) collective-permute-start(f32[1,32,32,128]{3,2,1,0:T(8,128)} %get-tuple-element.735), channel_id=1, source_target_pairs={{0,16},{16,32},{32,48},{48,64},{64,80},{80,96},{96,112},{112,128},... | collective-permute-start | bytes 1572872 | tf_op jit(solution)/shard_map/while/body/eval_jaxpr/ppermute | solution.py:13
  180.5 10.8 %collective-permute-start = (f32[1,32,32,128]{3,2,1,0:T(8,128)}, f32[1,32,32,128]{3,2,1,0:T(8,128)}, u32[]{:S(2)}, u32[]{:S(2)}) collective-permute-start(f32[1,32,32,128]{3,2,1,0:T(8,128)} %get-tuple-element.735), channel_id=1, source_target_pairs={{0,16},{16,32},{32,48},{48,64},{64,80},{80,96},{96,112},{112,128},... | collective-permute-start | bytes 1572872 | tf_op jit(solution)/shard_map/while/body/eval_jaxpr/ppermute | solution.py:13
  192.3 10.8 %collective-permute-start = (f32[1,32,32,128]{3,2,1,0:T(8,128)}, f32[1,32,32,128]{3,2,1,0:T(8,128)}, u32[]{:S(2)}, u32[]{:S(2)}) collective-permute-start(f32[1,32,32,128]{3,2,1,0:T(8,128)} %get-tuple-element.735), channel_id=1, source_target_pairs={{0,16},{16,32},{32,48},{48,64},{64,80},{80,96},{96,112},{112,128},... | collective-permute-start | bytes 1572872 | tf_op jit(solution)/shard_map/while/body/eval_jaxpr/ppermute | solution.py:13
  203.5 1.2 copy-start.13
  205.9 1.2 copy-start.15
  208.2 12.5 %copy-start.6 = (f32[1024,128]{1,0:T(8,128)}, f32[1024,128]{1,0:T(8,128)S(1)}, u32[]{:S(2)}) copy-start(f32[1024,128]{1,0:T(8,128)S(1)} %convolution_add_fusion.96) | copy-start | bytes 1572868
  208.4 1.2 copy-start.17
  208.4 2.3 copy-start.11
  210.7 7.3 %copy-start.4 = (f32[1024,128]{1,0:T(8,128)}, f32[1024,128]{1,0:T(8,128)S(1)}, u32[]{:S(2)}) copy-start(f32[1024,128]{1,0:T(8,128)S(1)} %convolution_add_fusion.88) | copy-start | bytes 1572868
  210.8 1.2 copy-start.19
  226.6 6.1 %collective-permute-start.1 = (bf16[1,32,32,128]{3,2,1,0:T(8,128)(2,1)}, bf16[1,32,32,128]{3,2,1,0:T(8,128)(2,1)S(1)}, u32[]{:S(2)}, u32[]{:S(2)}) collective-permute-start(bf16[1,32,32,128]{3,2,1,0:T(8,128)(2,1)} %copy-done.10), channel_id=1, source_target_pairs={{16,0},{32,16},{48,32},{64,48},{80,64},{96,80},{112,96},{128,112},... | collective-permute-start | bytes 786440 | tf_op jit(solution)/shard_map/while/body/eval_jaxpr/ppermute | solution.py:13
  233.6 7.9 %collective-permute-start.1 = (bf16[1,32,32,128]{3,2,1,0:T(8,128)(2,1)}, bf16[1,32,32,128]{3,2,1,0:T(8,128)(2,1)S(1)}, u32[]{:S(2)}, u32[]{:S(2)}) collective-permute-start(bf16[1,32,32,128]{3,2,1,0:T(8,128)(2,1)} %copy-done.10), channel_id=1, source_target_pairs={{16,0},{32,16},{48,32},{64,48},{80,64},{96,80},{112,96},{128,112},... | collective-permute-start | bytes 786440 | tf_op jit(solution)/shard_map/while/body/eval_jaxpr/ppermute | solution.py:13
  242.4 7.9 %collective-permute-start.1 = (bf16[1,32,32,128]{3,2,1,0:T(8,128)(2,1)}, bf16[1,32,32,128]{3,2,1,0:T(8,128)(2,1)S(1)}, u32[]{:S(2)}, u32[]{:S(2)}) collective-permute-start(bf16[1,32,32,128]{3,2,1,0:T(8,128)(2,1)} %copy-done.10), channel_id=1, source_target_pairs={{16,0},{32,16},{48,32},{64,48},{80,64},{96,80},{112,96},{128,112},... | collective-permute-start | bytes 786440 | tf_op jit(solution)/shard_map/while/body/eval_jaxpr/ppermute | solution.py:13
  251.2 9.0 %collective-permute-start.1 = (bf16[1,32,32,128]{3,2,1,0:T(8,128)(2,1)}, bf16[1,32,32,128]{3,2,1,0:T(8,128)(2,1)S(1)}, u32[]{:S(2)}, u32[]{:S(2)}) collective-permute-start(bf16[1,32,32,128]{3,2,1,0:T(8,128)(2,1)} %copy-done.10), channel_id=1, source_target_pairs={{16,0},{32,16},{48,32},{64,48},{80,64},{96,80},{112,96},{128,112},... | collective-permute-start | bytes 786440 | tf_op jit(solution)/shard_map/while/body/eval_jaxpr/ppermute | solution.py:13
  261.2 11.4 %collective-permute-start.1 = (bf16[1,32,32,128]{3,2,1,0:T(8,128)(2,1)}, bf16[1,32,32,128]{3,2,1,0:T(8,128)(2,1)S(1)}, u32[]{:S(2)}, u32[]{:S(2)}) collective-permute-start(bf16[1,32,32,128]{3,2,1,0:T(8,128)(2,1)} %copy-done.10), channel_id=1, source_target_pairs={{16,0},{32,16},{48,32},{64,48},{80,64},{96,80},{112,96},{128,112},... | collective-permute-start | bytes 786440 | tf_op jit(solution)/shard_map/while/body/eval_jaxpr/ppermute | solution.py:13
  273.5 9.8 %collective-permute-start.1 = (bf16[1,32,32,128]{3,2,1,0:T(8,128)(2,1)}, bf16[1,32,32,128]{3,2,1,0:T(8,128)(2,1)S(1)}, u32[]{:S(2)}, u32[]{:S(2)}) collective-permute-start(bf16[1,32,32,128]{3,2,1,0:T(8,128)(2,1)} %copy-done.10), channel_id=1, source_target_pairs={{16,0},{32,16},{48,32},{64,48},{80,64},{96,80},{112,96},{128,112},... | collective-permute-start | bytes 786440 | tf_op jit(solution)/shard_map/while/body/eval_jaxpr/ppermute | solution.py:13
  284.2 9.1 %collective-permute-start.1 = (bf16[1,32,32,128]{3,2,1,0:T(8,128)(2,1)}, bf16[1,32,32,128]{3,2,1,0:T(8,128)(2,1)S(1)}, u32[]{:S(2)}, u32[]{:S(2)}) collective-permute-start(bf16[1,32,32,128]{3,2,1,0:T(8,128)(2,1)} %copy-done.10), channel_id=1, source_target_pairs={{16,0},{32,16},{48,32},{64,48},{80,64},{96,80},{112,96},{128,112},... | collective-permute-start | bytes 786440 | tf_op jit(solution)/shard_map/while/body/eval_jaxpr/ppermute | solution.py:13
  294.3 9.1 %collective-permute-start.1 = (bf16[1,32,32,128]{3,2,1,0:T(8,128)(2,1)}, bf16[1,32,32,128]{3,2,1,0:T(8,128)(2,1)S(1)}, u32[]{:S(2)}, u32[]{:S(2)}) collective-permute-start(bf16[1,32,32,128]{3,2,1,0:T(8,128)(2,1)} %copy-done.10), channel_id=1, source_target_pairs={{16,0},{32,16},{48,32},{64,48},{80,64},{96,80},{112,96},{128,112},... | collective-permute-start | bytes 786440 | tf_op jit(solution)/shard_map/while/body/eval_jaxpr/ppermute | solution.py:13
  304.3 9.1 %collective-permute-start.1 = (bf16[1,32,32,128]{3,2,1,0:T(8,128)(2,1)}, bf16[1,32,32,128]{3,2,1,0:T(8,128)(2,1)S(1)}, u32[]{:S(2)}, u32[]{:S(2)}) collective-permute-start(bf16[1,32,32,128]{3,2,1,0:T(8,128)(2,1)} %copy-done.10), channel_id=1, source_target_pairs={{16,0},{32,16},{48,32},{64,48},{80,64},{96,80},{112,96},{128,112},... | collective-permute-start | bytes 786440 | tf_op jit(solution)/shard_map/while/body/eval_jaxpr/ppermute | solution.py:13
  314.4 9.1 %collective-permute-start.1 = (bf16[1,32,32,128]{3,2,1,0:T(8,128)(2,1)}, bf16[1,32,32,128]{3,2,1,0:T(8,128)(2,1)S(1)}, u32[]{:S(2)}, u32[]{:S(2)}) collective-permute-start(bf16[1,32,32,128]{3,2,1,0:T(8,128)(2,1)} %copy-done.10), channel_id=1, source_target_pairs={{16,0},{32,16},{48,32},{64,48},{80,64},{96,80},{112,96},{128,112},... | collective-permute-start | bytes 786440 | tf_op jit(solution)/shard_map/while/body/eval_jaxpr/ppermute | solution.py:13
  324.4 9.1 %collective-permute-start.1 = (bf16[1,32,32,128]{3,2,1,0:T(8,128)(2,1)}, bf16[1,32,32,128]{3,2,1,0:T(8,128)(2,1)S(1)}, u32[]{:S(2)}, u32[]{:S(2)}) collective-permute-start(bf16[1,32,32,128]{3,2,1,0:T(8,128)(2,1)} %copy-done.10), channel_id=1, source_target_pairs={{16,0},{32,16},{48,32},{64,48},{80,64},{96,80},{112,96},{128,112},... | collective-permute-start | bytes 786440 | tf_op jit(solution)/shard_map/while/body/eval_jaxpr/ppermute | solution.py:13
  334.4 9.1 %collective-permute-start.1 = (bf16[1,32,32,128]{3,2,1,0:T(8,128)(2,1)}, bf16[1,32,32,128]{3,2,1,0:T(8,128)(2,1)S(1)}, u32[]{:S(2)}, u32[]{:S(2)}) collective-permute-start(bf16[1,32,32,128]{3,2,1,0:T(8,128)(2,1)} %copy-done.10), channel_id=1, source_target_pairs={{16,0},{32,16},{48,32},{64,48},{80,64},{96,80},{112,96},{128,112},... | collective-permute-start | bytes 786440 | tf_op jit(solution)/shard_map/while/body/eval_jaxpr/ppermute | solution.py:13
  344.5 25.8 %collective-permute-start.1 = (bf16[1,32,32,128]{3,2,1,0:T(8,128)(2,1)}, bf16[1,32,32,128]{3,2,1,0:T(8,128)(2,1)S(1)}, u32[]{:S(2)}, u32[]{:S(2)}) collective-permute-start(bf16[1,32,32,128]{3,2,1,0:T(8,128)(2,1)} %copy-done.10), channel_id=1, source_target_pairs={{16,0},{32,16},{48,32},{64,48},{80,64},{96,80},{112,96},{128,112},... | collective-permute-start | bytes 786440 | tf_op jit(solution)/shard_map/while/body/eval_jaxpr/ppermute | solution.py:13
  372.6 1.0 copy-start.2
  374.5 6.1 %collective-permute-start.1 = (bf16[1,32,32,128]{3,2,1,0:T(8,128)(2,1)}, bf16[1,32,32,128]{3,2,1,0:T(8,128)(2,1)S(1)}, u32[]{:S(2)}, u32[]{:S(2)}) collective-permute-start(bf16[1,32,32,128]{3,2,1,0:T(8,128)(2,1)} %copy-done.10), channel_id=1, source_target_pairs={{16,0},{32,16},{48,32},{64,48},{80,64},{96,80},{112,96},{128,112},... | collective-permute-start | bytes 786440 | tf_op jit(solution)/shard_map/while/body/eval_jaxpr/ppermute | solution.py:13
  381.5 11.2 %collective-permute-start.1 = (bf16[1,32,32,128]{3,2,1,0:T(8,128)(2,1)}, bf16[1,32,32,128]{3,2,1,0:T(8,128)(2,1)S(1)}, u32[]{:S(2)}, u32[]{:S(2)}) collective-permute-start(bf16[1,32,32,128]{3,2,1,0:T(8,128)(2,1)} %copy-done.10), channel_id=1, source_target_pairs={{16,0},{32,16},{48,32},{64,48},{80,64},{96,80},{112,96},{128,112},... | collective-permute-start | bytes 786440 | tf_op jit(solution)/shard_map/while/body/eval_jaxpr/ppermute | solution.py:13
  396.0 1.0 copy-start.5
  396.0 1.2 copy-start.9
  396.0 1.3 copy-start.12
  398.5 1.2 copy-start.20
  410.4 1.1 copy-start.14
  462.0 1.0 copy-start.21
  (19 other events, 14.6 us)
Sparse Core Ops, SparseCore 0:
  417.8 130.9 all-gather.1
